TPU v7x, 32 devices: a whole 2x2x4 slice. The times are simulated.
32 devices in a mesh: groups: 2 (over x), ep: 16 (over z, y, core).
Axes of the slice: x: 2, y: 2, z: 4, core: 2. Of those that a mesh axis runs over, the one named last changes fastest.
Arguments:
- residual: bfloat16 [2048, 7168], P('groups', 'ep'), parts along dimension 0, may hold values from -6 to 6
- attn_out: bfloat16 [2048, 7168], P('groups', 'ep'), parts along dimension 0, may hold values from -6 to 6
- norm_gain: float32 [7168], replicated, may hold values from 0.5 to 1.5
- expert_routes: int32 [2048, 2], P(('groups', 'ep')), parts along dimension 0, may hold values from 0 to 2, as said below
- route_gain: float32 [2048, 2], P(('groups', 'ep')), parts along dimension 0, may hold values from 0.1 to 1
- w_gate: bfloat16 [7168, 4096], P(None, 'ep'), may hold values from -0.0625 to 0.0625
- w_up: bfloat16 [7168, 4096], P(None, 'ep'), may hold values from -0.0625 to 0.0625
- w_down: bfloat16 [4096, 7168], P('ep'), may hold values from -0.125 to 0.125
Outputs:
- mixed: bfloat16 [2048, 7168], P(('groups', 'ep')), parts along dimension 0
There are 2 independent parts, one for each index of `groups`. A program takes and returns all parts, laid end to end along the dimension named above; an argument that names none is the same for every part. Nothing has to cross between parts.
Inputs may be any that keep to these rules, and one draw needn't show every extreme that they name: `expert_routes`: value 2 marks a route to an expert outside this wave; a token names each expert of the wave at most once. Among the tokens of one block of 64, at most 64 routes name one expert, and in every draw some expert is named exactly 64 times by every block.
All inputs are finite; a program needn't handle non-finite values.
Results may differ from a plain program's by a relative error of at most 0.0055.
Values may be sent and summed in bfloat16 or wider, within the bound.
A program may use at most 192 MiB of HBM per device.

v0:
```python
import jax
import jax.numpy as jnp
from jax import lax
from jax.sharding import PartitionSpec as P

FSPLIT = 8
epsilon = 1e-06


def normalize(stream_rows, norm_gain):
    values = stream_rows.astype(jnp.float32)
    inv_rms = lax.rsqrt(jnp.mean(values * values, axis=-1, keepdims=True) + epsilon)
    return (values * inv_rms * norm_gain).astype(jnp.bfloat16)


def route_match(routes, experts, capacity):
    flat_ids = routes.reshape(-1)
    onehot = (flat_ids[:, None] == jnp.arange(experts, dtype=jnp.int32)[None, :]).astype(jnp.int32)
    earlier = jnp.cumsum(onehot, axis=0) - onehot
    slot_pos = jnp.sum(earlier * onehot, axis=1)
    slot_code = jnp.where(flat_ids < experts, flat_ids * capacity + slot_pos, -1)
    target = jnp.arange(experts * capacity, dtype=jnp.int32)
    return slot_code[None, :] == target[:, None]


def selection(routes, experts, capacity):
    matched = route_match(routes, experts, capacity).astype(jnp.int32)
    return matched.reshape(experts * capacity, routes.shape[0], routes.shape[1]).sum(axis=2)


def gain_table(routes, route_gain, experts, capacity):
    matched = route_match(routes, experts, capacity)
    weighted = jnp.where(matched, route_gain.reshape(-1)[None, :], 0.0)
    return weighted.reshape(experts * capacity, routes.shape[0], routes.shape[1]).sum(axis=2).T


def expert_rows(normed, w_gate, w_up, w_down):
    gate_act = jnp.dot(normed, w_gate, preferred_element_type=jnp.float32)
    up_act = jnp.dot(normed, w_up, preferred_element_type=jnp.float32)
    hidden = (jax.nn.silu(gate_act) * up_act).astype(jnp.bfloat16)
    return jnp.dot(hidden, w_down, preferred_element_type=jnp.float32).astype(jnp.bfloat16)


def body(residual, attn_out, norm_gain, expert_routes, route_gain, w_gate, w_up, w_down):
    devices = lax.axis_size("ep")
    tok_here = expert_routes.shape[0]
    route_slots = expert_routes.shape[1]
    experts = devices // FSPLIT
    capacity = route_slots * tok_here // experts
    model_width = w_gate.shape[0]
    stream_feat = (residual.astype(jnp.float32) + attn_out.astype(jnp.float32)).astype(jnp.bfloat16)
    stream_rows = lax.all_to_all(stream_feat, "ep", split_axis=0, concat_axis=1, tiled=True)
    combine_weights = gain_table(expert_routes, route_gain, experts, capacity)
    normed_rows = normalize(stream_rows, norm_gain)
    select = selection(expert_routes, experts, capacity).astype(jnp.bfloat16)
    per_expert = jnp.dot(select, normed_rows, preferred_element_type=jnp.float32).astype(
        jnp.bfloat16
    )
    per_expert = per_expert.reshape(experts, 1, capacity, model_width)
    outgoing = jnp.broadcast_to(per_expert, (experts, FSPLIT, capacity, model_width))
    outgoing = outgoing.reshape(devices, capacity, model_width)
    received = lax.all_to_all(outgoing, "ep", split_axis=0, concat_axis=0, tiled=True)
    slot_count = received.shape[1]
    partial_value = expert_rows(received.reshape(-1, model_width), w_gate, w_up, w_down)
    partial_value = partial_value.reshape(devices, slot_count, model_width)
    returned = lax.all_to_all(partial_value, "ep", split_axis=0, concat_axis=0, tiled=True)
    summed = (
        returned.reshape(experts, FSPLIT, capacity, model_width).astype(jnp.float32).sum(axis=1)
    )
    summed = summed.reshape(experts * capacity, model_width)
    routed_sum = jnp.dot(combine_weights, summed, precision=lax.Precision.HIGHEST)
    return (stream_rows.astype(jnp.float32) + routed_sum).astype(jnp.bfloat16)


def dense_body(residual, attn_out, norm_gain, expert_routes, route_gain, w_gate, w_up, w_down):
    devices = lax.axis_size("ep")
    rank = lax.axis_index("ep")
    tok_here = expert_routes.shape[0]
    experts = devices // FSPLIT
    stream_feat = (residual.astype(jnp.float32) + attn_out.astype(jnp.float32)).astype(jnp.bfloat16)
    named = jnp.arange(experts, dtype=jnp.int32)
    gains = jnp.sum(
        jnp.where(expert_routes[:, :, None] == named, route_gain[:, :, None], 0.0), axis=1
    )
    all_gains = lax.all_gather(gains, "ep", axis=0, tiled=True)
    here = (rank // FSPLIT == named).astype(jnp.float32)
    gain_here = jnp.sum(all_gains * here, axis=1, keepdims=True)
    stream = lax.all_gather(stream_feat, "ep", axis=1, tiled=True)
    normed = normalize(stream, norm_gain)
    gate_act = jnp.dot(normed, w_gate, preferred_element_type=jnp.float32)
    up_act = jnp.dot(normed, w_up, preferred_element_type=jnp.float32)
    hidden = (jax.nn.silu(gate_act) * up_act * gain_here).astype(jnp.bfloat16)
    partial = jnp.dot(hidden, w_down, preferred_element_type=jnp.float32).astype(jnp.bfloat16)
    routed = lax.psum_scatter(partial, "ep", scatter_dimension=0, tiled=True)
    own = lax.dynamic_slice_in_dim(stream, rank * tok_here, tok_here, 0)
    return (own.astype(jnp.float32) + routed.astype(jnp.float32)).astype(jnp.bfloat16)


def pick_body(residual, attn_out, norm_gain, expert_routes, route_gain, w_gate, w_up, w_down):
    experts = lax.axis_size("ep") // FSPLIT
    capacity = expert_routes.shape[1] * expert_routes.shape[0] // experts
    run = dense_body if capacity >= expert_routes.shape[0] else body
    return run(residual, attn_out, norm_gain, expert_routes, route_gain, w_gate, w_up, w_down)


def solution(mesh):
    in_specs = (
        P("groups", "ep"),
        P("groups", "ep"),
        P(),
        P(("groups", "ep"), None),
        P(("groups", "ep"), None),
        P(None, "ep"),
        P(None, "ep"),
        P("ep", None),
    )
    out_specs = P(("groups", "ep"), None)
    return jax.shard_map(
        pick_body, mesh=mesh, in_specs=in_specs, out_specs=out_specs, check_vma=False
    )
```

profile of v0, /device:TPU:0, one launch (start us, length us, event | category | flops | bytes accessed | tf_op | source)
XLA Modules:
  0.0 322.8 jit_solution(7956764136521179954)
XLA Ops:
  6.5 0.0 copy-start.1
  6.5 0.0 all-gather.3.cloned.1.call-start
  6.5 2.7 add_convert_fusion.1
  9.3 0.0 all-gather.3.cloned.1.call-update
  9.3 0.0 reduce-scatter.2.cloned.1.call-start
  9.4 0.7 fusion.23
  10.1 23.6 %all-gather = f32[16,64,2]{1,2,0:T(2,128)S(1)} all-gather(f32[1,64,2]{1,2,0:T(2,128)S(1)} %bitcast.11), channel_id=1, replica_groups=mesh['groups'=2,'ep'=16] {'ep'}, dimensions={0}, use_global_device_ids=true | all-gather | bytes 8704 | tf_op jit(solution)/shard_map/all_gather | solution.py:85
  33.7 0.1 reshape.18
  33.8 0.1 multiply_reduce_fusion
  33.9 91.9 %all-gather.3.cloned.1.call-done = bf16[1024,7168]{0,1:T(8,128)(2,1)} async-done(((bf16[1024,448]{0,1:T(8,128)(2,1)}), bf16[1024,7168]{0,1:T(8,128)(2,1)}) %all-gather.3.cloned.1.call-update) | async-done | bytes 14680080 | tf_op jit(solution)/shard_map/all_gather | solution.py:88
  125.8 8.1 %fusion = f32[1024]{0:T(1024)S(1)} fusion(bf16[1024,7168]{0,1:T(8,128)(2,1)} %all-gather.3.cloned.1.call-done), kind=kLoop, calls=%fused_computation.2 | loop fusion | flops 22019072 | bytes 14684160 | tf_op jit(solution)/shard_map/reduce_sum | solution.py:12
  133.8 0.0 copy-done.1
  133.9 0.0 copy-start
  133.9 12.8 %fusion.5 = f32[1024,256]{1,0:T(8,128)} fusion(bf16[7168,256]{1,0:T(8,128)(2,1)} %param.13, bf16[1024,7168]{0,1:T(8,128)(2,1)} %all-gather.3.cloned.1.call-done, f32[7168]{0:T(1024)S(1)} %copy-done.1, f32[1024]{0:T(1024)S(1)} %add_rsqrt_fusion), kind=kOutput, calls=%fused_computation.7 | convolution fusion | flops 3787456512 | bytes 19431424 | tf_op jit(solution)/shard_map/dot_general | solution.py:90
  146.6 0.0 copy-done
  146.6 9.2 %fusion.13.clone.4 = bf16[1024,256]{1,0:T(8,128)(2,1)S(1)} fusion(bf16[7168,256]{1,0:T(8,128)(2,1)} %param.14, bf16[1024,7168]{0,1:T(8,128)(2,1)S(1)} %copy-done, f32[7168]{0:T(1024)S(1)} %copy-done.1, f32[1024]{0:T(1024)S(1)} %add_rsqrt_fusion, f32[1024,256]{1,0:T(8,128)} %fusion.5, f32[1024]{0:T(1024)S(1)} %multiply_reduce_fusion), kind=kOutput, calls=%fused_computation.12.clone.clone.clone.1 | convolution fusion | flops 3789291520 | bytes 19959808 | tf_op jit(solution)/shard_map/dot_general | solution.py:91
  155.8 9.3 %convolution_convert_fusion = bf16[1024,7168]{1,0:T(8,128)(2,1)} fusion(bf16[256,7168]{1,0:T(8,128)(2,1)} %param.15, bf16[1024,256]{1,0:T(8,128)(2,1)S(1)} %fusion.13.clone.4), kind=kOutput, calls=%fused_computation.5 | convolution fusion | flops 3765436416 | bytes 18874368 | tf_op jit(solution)/shard_map/dot_general | solution.py:93
  165.1 0.0 reduce-scatter.2.cloned.1.call-update
  165.2 2.1 constant_dynamic-slice_fusion
  167.2 0.8 copy.24
  168.0 145.6 %reduce-scatter.2.cloned.1.call-done = bf16[64,7168]{1,0:T(8,128)(2,1)} async-done(((bf16[1024,7168]{1,0:T(8,128)(2,1)}), bf16[64,7168]{1,0:T(8,128)(2,1)}) %reduce-scatter.2.cloned.1.call-update) | async-done | bytes 917520 | tf_op jit(solution)/shard_map/reduce_scatter | solution.py:94
  313.6 2.3 add_convert_fusion
  (3 shorter events, 0.0 us)
Async XLA Ops:
  6.5 127.3 %copy-start.1 = (f32[7168]{0:T(1024)S(1)}, f32[7168]{0:T(1024)}, u32[]{:S(2)}) copy-start(f32[7168]{0:T(1024)} %param.10) | copy-start | bytes 86020
  6.5 119.2 %all-gather.3.cloned.1.call-start = ((), (), s32[]{:S(2)}) async-start(), calls=%async_computation.1 | async-start | bytes 15597568 | tf_op jit(solution)/shard_map/all_gather | solution.py:88
  9.3 304.3 %reduce-scatter.2.cloned.1.call-start = ((), (), s32[]{:S(2)}) async-start(), calls=%async_computation.2 | async-start | bytes 15597568 | tf_op jit(solution)/shard_map/reduce_scatter | solution.py:94
  133.9 12.8 %copy-start = (bf16[1024,7168]{0,1:T(8,128)(2,1)S(1)}, bf16[1024,7168]{0,1:T(8,128)(2,1)}, u32[]{:S(2)}) copy-start(bf16[1024,7168]{0,1:T(8,128)(2,1)} %all-gather.3.cloned.1.call-done) | copy-start | bytes 44040196
Sparse Core Ops, SparseCore 0:
  9.6 116.0 all-gather.2
  165.3 148.2 reduce-scatter.1
where the time goes:
time: 323 us
  waiting for transfers between devices  238 us (74%)
  matrix products  31.3 us (10%)
  blocking collectives  23.6 us (7%)
  other arithmetic  13.9 us (4%)
  between operations  13.5 us (4%)
    reduce_scatter x1, waiting for transfers between devices, dense_body(): routed = lax.psum_scatter(partial, 'ep', scatter_dimension=0, tiled=True)  146 us
    all_gather x1, waiting for transfers between devices, dense_body(): stream = lax.all_gather(stream_feat, 'ep', axis=1, tiled=True)  91.9 us
    all_gather x1, blocking collectives, dense_body(): all_gains = lax.all_gather(gains, 'ep', axis=0, tiled=True)  23.6 us
    dot_general x1, matrix products, dense_body(): gate_act = jnp.dot(normed, w_gate, preferred_element_type=jnp.float32)  12.8 us
    dot_general x1, matrix products, dense_body(): jnp.dot(hidden, w_down, preferred_element_type=jnp.float32)  9.34 us
    dot_general x1, matrix products, dense_body(): up_act = jnp.dot(normed, w_up, preferred_element_type=jnp.float32)  9.16 us
    reduce_sum x1, other arithmetic, normalize(): jnp.mean(values * values, axis=-1, keepdims=True) + epsilon  8.08 us
  transfers between devices with their start and end apart: 2, of which 2 were waited for; matrix products, arithmetic and copies ran while one was open for 1% of the time, Pallas kernels for 0%

commit v1 on v0

--- a/solution.py
+++ b/solution.py
@@ -85,7 +85,9 @@
     all_gains = lax.all_gather(gains, "ep", axis=0, tiled=True)
     here = (rank // FSPLIT == named).astype(jnp.float32)
     gain_here = jnp.sum(all_gains * here, axis=1, keepdims=True)
-    stream = lax.all_gather(stream_feat, "ep", axis=1, tiled=True)
+    stream = jnp.concatenate(
+        lax.all_to_all(jnp.stack([stream_feat] * lax.axis_size("ep")), "ep", 0, 0), axis=1
+    )
     normed = normalize(stream, norm_gain)
     gate_act = jnp.dot(normed, w_gate, preferred_element_type=jnp.float32)
     up_act = jnp.dot(normed, w_up, preferred_element_type=jnp.float32)

time: 323 us -> 548 us (1.70)
  blocking collectives: 23.6 us -> 252 us
  waiting for transfers between devices: 238 us -> 222 us
  starting transfers between devices: 0.04 us -> 7.63 us
  local copies, waits for them, and re-layouts: 2.91 us -> 10 us
    all_gather x1, blocking collectives: 23.6 us -> 252 us  [dense_body(): all_gains = lax.all_gather(gains, 'ep', axis=0, tiled=True)]
    all_gather x1 -> x0, waiting for transfers between devices: 91.9 us -> none  [dense_body(): stream = lax.all_gather(stream_feat, 'ep', axis=1, tiled=True)]
    reduce_scatter x1, waiting for transfers between devices: 146 us -> 214 us  [dense_body(): routed = lax.psum_scatter(partial, 'ep', scatter_dimension=0, tiled=True)]
    all_to_all x0 -> x1, starting transfers between devices: none -> 7.59 us  [dense_body(): lax.all_to_all(jnp.stack([stream_feat] * lax.axis_size('ep')), 'ep', 0, 0)]
    all_to_all x0 -> x1, waiting for transfers between devices: none -> 7.49 us  [dense_body(): lax.all_to_all(jnp.stack([stream_feat] * lax.axis_size('ep')), 'ep', 0, 0)]
    another operation x0 -> x1, local copies, waits for them, and re-layouts: none -> 7.09 us  [dense_body(): jnp.stack([stream_feat] * lax.axis_size('ep'))]
where the time goes in v1:
time: 548 us; the launch traced here: 547 us
  blocking collectives  252 us (46%)
  waiting for transfers between devices  222 us (41%)
  matrix products  29.6 us (5%)
  between operations  13.5 us (2%)
  other arithmetic  12.3 us (2%)
  local copies, waits for them, and re-layouts  10 us (2%)
  starting transfers between devices  7.63 us (1%)
    all_gather x1, blocking collectives, dense_body(): all_gains = lax.all_gather(gains, 'ep', axis=0, tiled=True)  252 us
    reduce_scatter x1, waiting for transfers between devices, dense_body(): routed = lax.psum_scatter(partial, 'ep', scatter_dimension=0, tiled=True)  214 us
    dot_general x1, matrix products, dense_body(): gate_act = jnp.dot(normed, w_gate, preferred_element_type=jnp.float32)  11.8 us
  transfers between devices with their start and end apart: 2, of which 2 were waited for; matrix products, arithmetic and copies ran while one was open for 1% of the time, Pallas kernels for 0%

profile of v1, /device:TPU:0, one launch (start us, length us, event | category | flops | bytes accessed | tf_op | source)
XLA Modules:
  0.0 547.2 jit_solution(7529189466386126376)
XLA Ops:
  6.5 1.8 add_convert_fusion.1
  8.3 7.1 %stack.2 = bf16[16,1024,448]{1,2,0:T(8,128)(2,1)} broadcast(bf16[1024,448]{0,1:T(8,128)(2,1)S(1)} %add_convert_fusion.1), dimensions={1,2} | broadcast | bytes 15597568 | tf_op jit(solution)/shard_map/stack | solution.py:89
  15.4 0.0 copy-start.1
  15.4 0.0 copy-start.2
  15.4 7.6 %all-to-all-start = ((bf16[16,1024,448]{1,2,0:T(8,128)(2,1)}), bf16[16,1024,448]{1,2,0:T(8,128)(2,1)}, u32[]{:S(2)}, u32[]{:S(2)}) async-start(bf16[16,1024,448]{1,2,0:T(8,128)(2,1)} %stack.2), calls=%async_computation | async-start | bytes 29360128 | tf_op jit(solution)/shard_map/all_to_all | solution.py:89
  23.0 0.0 copy-start.4
  23.0 0.0 reduce-scatter.2.cloned.1.call-start
  23.1 0.0 copy-done.1
  23.1 0.0 copy-done.2
  23.1 252.5 %all-gather = f32[16,64,2]{1,2,0:T(2,128)S(1)} all-gather(f32[1,64,2]{1,2,0:T(2,128)S(1)} %bitcast.15), channel_id=1, replica_groups=mesh['groups'=2,'ep'=16] {'ep'}, dimensions={0}, use_global_device_ids=true | all-gather | bytes 8704 | tf_op jit(solution)/shard_map/all_gather | solution.py:85
  275.6 0.1 reshape.28
  275.7 0.1 multiply_reduce_fusion.1
  275.8 7.5 %all-to-all-done = bf16[16,1024,448]{1,2,0:T(8,128)(2,1)} async-done(((bf16[16,1024,448]{1,2,0:T(8,128)(2,1)}), bf16[16,1024,448]{1,2,0:T(8,128)(2,1)}, u32[]{:S(2)}, u32[]{:S(2)}) %all-to-all-start) | async-done | bytes 14680096 | tf_op jit(solution)/shard_map/all_to_all | solution.py:89
  283.3 8.1 %multiply_reduce_fusion = f32[1024]{0:T(1024)S(1)} fusion(bf16[16,1024,448]{1,2,0:T(8,128)(2,1)} %all-to-all-done), kind=kLoop, calls=%fused_computation.1 | loop fusion | flops 22019072 | bytes 14684160 | tf_op jit(solution)/shard_map/reduce_sum | solution.py:12
  291.4 0.0 copy-done.4
  291.4 0.0 copy-start.3
  291.4 11.8 %fusion.1 = f32[1024,256]{1,0:T(8,128)S(1)} fusion(bf16[7168,256]{1,0:T(8,128)(2,1)} %param.13, bf16[1024,7168]{0,1:T(8,128)(2,1)} %bitcast.1, f32[7168]{0:T(1024)S(1)} %copy-done.4, f32[1024]{0:T(1024)S(1)} %add_rsqrt_fusion), kind=kOutput, calls=%fused_computation.4 | convolution fusion | flops 3787456512 | bytes 19431424 | tf_op jit(solution)/shard_map/dot_general | solution.py:92
  303.1 0.0 copy-done.3
  303.2 0.0 copy-start
  303.2 10.6 %fusion.4.clone.4 = bf16[1024,256]{1,0:T(8,128)(2,1)S(1)} fusion(bf16[7168,256]{1,0:T(8,128)(2,1)S(1)} %copy-done.3, bf16[1024,7168]{0,1:T(8,128)(2,1)} %bitcast.1, f32[7168]{0:T(1024)S(1)} %copy-done.4, f32[1024]{0:T(1024)S(1)} %add_rsqrt_fusion, f32[1024,256]{1,0:T(8,128)S(1)} %fusion.1, f32[1024]{0:T(1024)S(1)} %multiply_reduce_fusion.1), kind=kOutput, calls=%fused_computation.9.clone.clone.clone.1 | convolution fusion | flops 3789291520 | bytes 19959808 | tf_op jit(solution)/shard_map/dot_general | solution.py:93
  313.8 0.0 copy-done
  313.8 7.3 %convolution_convert_fusion = bf16[1024,7168]{1,0:T(8,128)(2,1)} fusion(bf16[256,7168]{1,0:T(8,128)(2,1)S(1)} %copy-done, bf16[1024,256]{1,0:T(8,128)(2,1)S(1)} %fusion.4.clone.4), kind=kOutput, calls=%fused_computation.2 | convolution fusion | flops 3765436416 | bytes 18874368 | tf_op jit(solution)/shard_map/dot_general | solution.py:95
  321.1 0.0 reduce-scatter.2.cloned.1.call-update
  321.1 2.1 constant_dynamic-slice_fusion
  323.2 0.8 copy.22
  323.9 214.1 %reduce-scatter.2.cloned.1.call-done = bf16[64,7168]{1,0:T(8,128)(2,1)} async-done(((bf16[1024,7168]{1,0:T(8,128)(2,1)}), bf16[64,7168]{1,0:T(8,128)(2,1)}) %reduce-scatter.2.cloned.1.call-update) | async-done | bytes 917520 | tf_op jit(solution)/shard_map/reduce_scatter | solution.py:96
  538.1 2.3 add_convert_fusion
  (4 shorter events, 0.0 us)
Async XLA Ops:
  15.4 7.7 %copy-start.1 = (f32[64,2]{0,1:T(2,128)S(1)}, f32[64,2]{0,1:T(2,128)}, u32[]{:S(2)}) copy-start(f32[64,2]{0,1:T(2,128)} %param.12) | copy-start | bytes 1540
  15.4 7.7 %copy-start.2 = (s32[64,2]{0,1:T(2,128)S(1)}, s32[64,2]{0,1:T(2,128)}, u32[]{:S(2)}) copy-start(s32[64,2]{0,1:T(2,128)} %param.11) | copy-start | bytes 1540
  15.4 267.8 %all-to-all-start = ((bf16[16,1024,448]{1,2,0:T(8,128)(2,1)}), bf16[16,1024,448]{1,2,0:T(8,128)(2,1)}, u32[]{:S(2)}, u32[]{:S(2)}) async-start(bf16[16,1024,448]{1,2,0:T(8,128)(2,1)} %stack.2), calls=%async_computation | async-start | bytes 29360128 | tf_op jit(solution)/shard_map/all_to_all | solution.py:89
  23.0 268.3 %copy-start.4 = (f32[7168]{0:T(1024)S(1)}, f32[7168]{0:T(1024)}, u32[]{:S(2)}) copy-start(f32[7168]{0:T(1024)} %param.10) | copy-start | bytes 86020
  23.0 515.0 %reduce-scatter.2.cloned.1.call-start = ((), (), s32[]{:S(2)}) async-start(), calls=%async_computation.2 | async-start | bytes 15597568 | tf_op jit(solution)/shard_map/reduce_scatter | solution.py:96
  291.4 11.8 %copy-start.3 = (bf16[7168,256]{1,0:T(8,128)(2,1)S(1)}, bf16[7168,256]{1,0:T(8,128)(2,1)}, u32[]{:S(2)}) copy-start(bf16[7168,256]{1,0:T(8,128)(2,1)} %param.14) | copy-start | bytes 11010052
  303.2 10.6 %copy-start = (bf16[256,7168]{1,0:T(8,128)(2,1)S(1)}, bf16[256,7168]{1,0:T(8,128)(2,1)}, u32[]{:S(2)}) copy-start(bf16[256,7168]{1,0:T(8,128)(2,1)} %param.15) | copy-start | bytes 11010052
Sparse Core Ops, SparseCore 0:
  321.2 216.8 reduce-scatter.1
